TPU v7x, 256 devices: a whole 4x4x8 slice. The times are simulated.
256 devices in a mesh: graph: 32 (over z, x_hi, core), feat: 8 (over x_lo, y).
Axes of the slice: x: 4 (x_hi: 2, x_lo: 2; x = x_hi * 2 + x_lo), y: 4, z: 8, core: 2. Of those that a mesh axis runs over, the one named last changes fastest.
Arguments:
- features: bfloat16 [256, 65536], P('feat', 'graph'), may hold values from -6 to 6
- tiles: bfloat16 [8192, 128, 128], P('graph'), may hold values from 0 to 0.049316406
- tile_source: int32 [8192], P('graph'), may hold values from 0 to 511, as said below
- tile_target: int32 [8192], P('graph'), may hold values from 0 to 15
- tile_count: int32 [32], P('graph'), may hold values from 88 to 256, as said below
- weight: bfloat16 [256, 256], replicated, may hold values from -0.375 to 0.375
Outputs:
- layer_output: bfloat16 [256, 65536], P('feat', 'graph')
Inputs may be any that keep to these rules, and one draw needn't show every extreme that they name: Within the 256 slots of each slab, the source slab tile_source // 16 never falls from one slot to the next. The used slots of a slab hold at least one tile from every slab's node blocks and at most 16 from any one slab's, and exactly 16 from some slab's, on every slab. `tile_count`: some slab uses all 256 slots.
All inputs are finite; a program needn't handle non-finite values.
Results may differ from a plain program's by a relative error of at most 0.0049.
Values may be sent and summed in bfloat16 or wider, within the bound.
No kernel may reach another device: no remote copies, remote signals or barrier semaphores. Data moves between devices by JAX's collectives and lax.ppermute only.
A program may use at most 64 MiB of HBM per device.

v0:
```python
import jax
import jax.numpy as jnp
from jax import lax
from jax.sharding import PartitionSpec as P

PAIR_MOST = 16


def shifted(block, axis, distance):
    devices = range(lax.axis_size(axis))
    route = [((i - distance) % len(devices), i) for i in devices]
    return lax.ppermute(block, axis, route)


def add_tiles(totals, visitor, tile_group, source_blocks, target_blocks, keep_mask):
    feature_rows = visitor.shape[0]
    tile_side = tile_group.shape[1]
    blocks = visitor.reshape(feature_rows, -1, tile_side)
    picked = jnp.take(blocks, source_blocks, axis=1)
    products = jnp.einsum("hwj,wij->hwi", picked, tile_group, preferred_element_type=jnp.float32)
    masked = products * keep_mask.astype(jnp.float32)[None, :, None]
    return totals.at[:, target_blocks, :].add(masked)


def body(features, tiles, tile_source, tile_target, tile_count, weight):
    slab_count = lax.axis_size("graph")
    position = lax.axis_index("graph")
    feature_rows, slab_nodes = features.shape
    tile_side = tiles.shape[1]
    block_count = slab_nodes // tile_side
    slot_total = tiles.shape[0]
    usable = jnp.arange(slot_total) < tile_count[0]
    source_slab = tile_source // block_count
    local_source = tile_source % block_count
    zero_totals = jnp.zeros((feature_rows, block_count, tile_side), jnp.float32)

    def add_slab(totals, visitor, slab_index):
        before = jnp.sum(((source_slab < slab_index) & usable).astype(jnp.int32))
        first_slot = jnp.minimum(before, slot_total - PAIR_MOST)
        window = lax.dynamic_slice_in_dim(tiles, first_slot, PAIR_MOST, 0)
        sources = lax.dynamic_slice_in_dim(local_source, first_slot, PAIR_MOST, 0)
        targets = lax.dynamic_slice_in_dim(tile_target, first_slot, PAIR_MOST, 0)
        keep_mask = lax.dynamic_slice_in_dim(
            (source_slab == slab_index) & usable, first_slot, PAIR_MOST, 0
        )
        return add_tiles(totals, visitor, window, sources, targets, keep_mask)

    def forward_turn(turn_index, running):
        totals, visitor = running
        visitor = shifted(visitor, "graph", 1)
        return (add_slab(totals, visitor, (position - turn_index) % slab_count), visitor)

    totals, last_visitor = lax.fori_loop(
        1, slab_count, forward_turn, (add_slab(zero_totals, features, position), features)
    )
    rounded = totals.reshape(feature_rows, slab_nodes).astype(jnp.bfloat16)
    columns = lax.dynamic_slice_in_dim(
        weight, lax.axis_index("feat") * feature_rows, feature_rows, 1
    )
    combined = jnp.einsum(
        "ko,kn->on",
        columns,
        lax.all_gather(rounded, "feat", axis=0, tiled=True),
        preferred_element_type=jnp.float32,
    )
    return jnp.maximum(combined, 0.0).astype(jnp.bfloat16)


def solution(mesh):
    return jax.shard_map(
        body,
        mesh=mesh,
        in_specs=(
            P("feat", "graph"),
            P("graph", None, None),
            P("graph"),
            P("graph"),
            P("graph"),
            P(),
        ),
        out_specs=P("feat", "graph"),
        check_vma=False,
    )
```

profile of v0, /device:TPU:4, one launch (start us, length us, event | category | flops | bytes accessed | tf_op | source)
XLA Modules:
  0.0 421.0 jit_solution(14925830925300414950)
XLA Ops:
  15.0 344.0 %while.18 = (s32[]{:T(128)}, f32[32,16,128]{2,0,1:T(8,128)S(1)}, bf16[32,2048]{1,0:T(8,128)(2,1)S(1)}, s32[]{:T(128)}, s32[256]{0:T(256)S(1)}, /*index=5*/s32[25...) while((s32[]{:T(128)}, f32[32,16,128]{2,0,1:T(8,128)S(1)}, ...), condition=%wide.region_5.7_spmd.clone, body=%wide.region_2.6_spmd.clone.sunk | while | flops 16977072 | bytes 3022064 | solution.py:53
  18.5 2.5 collective-permute-done
  21.6 1.5 fusion.35
  27.8 2.5 collective-permute-done
  30.9 1.5 fusion.35
  37.5 2.1 collective-permute-done
  40.2 1.5 fusion.35
  49.4 1.5 fusion.35
  52.2 2.3 collective-permute-start
  59.8 1.5 fusion.35
  62.5 2.1 collective-permute-start
  68.0 2.5 collective-permute-done
  71.2 1.5 fusion.35
  78.2 3.8 collective-permute-done
  82.6 1.5 fusion.35
  88.8 4.6 %collective-permute-done = bf16[32,2048]{1,0:T(8,128)(2,1)S(1)} collective-permute-done((bf16[32,2048]{1,0:T(8,128)(2,1)S(1)}, bf16[32,2048]{1,0:T(8,128)(2,1)S(1)}, u32[]{:S(2)}, u32[]{:S(2)}) %collective-permute-start) | collective-permute-done | bytes 131104 | tf_op jit(solution)/shard_map/while/body/eval_jaxpr/ppermute | solution.py:12
  94.0 1.5 fusion.35
  100.2 4.6 %collective-permute-done = bf16[32,2048]{1,0:T(8,128)(2,1)S(1)} collective-permute-done((bf16[32,2048]{1,0:T(8,128)(2,1)S(1)}, bf16[32,2048]{1,0:T(8,128)(2,1)S(1)}, u32[]{:S(2)}, u32[]{:S(2)}) %collective-permute-start) | collective-permute-done | bytes 131104 | tf_op jit(solution)/shard_map/while/body/eval_jaxpr/ppermute | solution.py:12
  105.4 1.5 fusion.35
  111.6 4.6 %collective-permute-done = bf16[32,2048]{1,0:T(8,128)(2,1)S(1)} collective-permute-done((bf16[32,2048]{1,0:T(8,128)(2,1)S(1)}, bf16[32,2048]{1,0:T(8,128)(2,1)S(1)}, u32[]{:S(2)}, u32[]{:S(2)}) %collective-permute-start) | collective-permute-done | bytes 131104 | tf_op jit(solution)/shard_map/while/body/eval_jaxpr/ppermute | solution.py:12
  116.8 1.5 fusion.35
  123.0 4.6 %collective-permute-done = bf16[32,2048]{1,0:T(8,128)(2,1)S(1)} collective-permute-done((bf16[32,2048]{1,0:T(8,128)(2,1)S(1)}, bf16[32,2048]{1,0:T(8,128)(2,1)S(1)}, u32[]{:S(2)}, u32[]{:S(2)}) %collective-permute-start) | collective-permute-done | bytes 131104 | tf_op jit(solution)/shard_map/while/body/eval_jaxpr/ppermute | solution.py:12
  128.2 1.5 fusion.35
  134.4 4.6 %collective-permute-done = bf16[32,2048]{1,0:T(8,128)(2,1)S(1)} collective-permute-done((bf16[32,2048]{1,0:T(8,128)(2,1)S(1)}, bf16[32,2048]{1,0:T(8,128)(2,1)S(1)}, u32[]{:S(2)}, u32[]{:S(2)}) %collective-permute-start) | collective-permute-done | bytes 131104 | tf_op jit(solution)/shard_map/while/body/eval_jaxpr/ppermute | solution.py:12
  139.6 1.5 fusion.35
  145.8 4.6 %collective-permute-done = bf16[32,2048]{1,0:T(8,128)(2,1)S(1)} collective-permute-done((bf16[32,2048]{1,0:T(8,128)(2,1)S(1)}, bf16[32,2048]{1,0:T(8,128)(2,1)S(1)}, u32[]{:S(2)}, u32[]{:S(2)}) %collective-permute-start) | collective-permute-done | bytes 131104 | tf_op jit(solution)/shard_map/while/body/eval_jaxpr/ppermute | solution.py:12
  151.0 1.5 fusion.35
  157.2 4.6 %collective-permute-done = bf16[32,2048]{1,0:T(8,128)(2,1)S(1)} collective-permute-done((bf16[32,2048]{1,0:T(8,128)(2,1)S(1)}, bf16[32,2048]{1,0:T(8,128)(2,1)S(1)}, u32[]{:S(2)}, u32[]{:S(2)}) %collective-permute-start) | collective-permute-done | bytes 131104 | tf_op jit(solution)/shard_map/while/body/eval_jaxpr/ppermute | solution.py:12
  162.4 1.5 fusion.35
  168.6 4.6 %collective-permute-done = bf16[32,2048]{1,0:T(8,128)(2,1)S(1)} collective-permute-done((bf16[32,2048]{1,0:T(8,128)(2,1)S(1)}, bf16[32,2048]{1,0:T(8,128)(2,1)S(1)}, u32[]{:S(2)}, u32[]{:S(2)}) %collective-permute-start) | collective-permute-done | bytes 131104 | tf_op jit(solution)/shard_map/while/body/eval_jaxpr/ppermute | solution.py:12
  173.8 1.5 fusion.35
  180.0 4.6 %collective-permute-done = bf16[32,2048]{1,0:T(8,128)(2,1)S(1)} collective-permute-done((bf16[32,2048]{1,0:T(8,128)(2,1)S(1)}, bf16[32,2048]{1,0:T(8,128)(2,1)S(1)}, u32[]{:S(2)}, u32[]{:S(2)}) %collective-permute-start) | collective-permute-done | bytes 131104 | tf_op jit(solution)/shard_map/while/body/eval_jaxpr/ppermute | solution.py:12
  185.2 1.5 fusion.35
  191.4 4.6 %collective-permute-done = bf16[32,2048]{1,0:T(8,128)(2,1)S(1)} collective-permute-done((bf16[32,2048]{1,0:T(8,128)(2,1)S(1)}, bf16[32,2048]{1,0:T(8,128)(2,1)S(1)}, u32[]{:S(2)}, u32[]{:S(2)}) %collective-permute-start) | collective-permute-done | bytes 131104 | tf_op jit(solution)/shard_map/while/body/eval_jaxpr/ppermute | solution.py:12
  196.6 1.5 fusion.35
  202.8 4.6 %collective-permute-done = bf16[32,2048]{1,0:T(8,128)(2,1)S(1)} collective-permute-done((bf16[32,2048]{1,0:T(8,128)(2,1)S(1)}, bf16[32,2048]{1,0:T(8,128)(2,1)S(1)}, u32[]{:S(2)}, u32[]{:S(2)}) %collective-permute-start) | collective-permute-done | bytes 131104 | tf_op jit(solution)/shard_map/while/body/eval_jaxpr/ppermute | solution.py:12
  208.0 1.5 fusion.35
  214.2 4.6 %collective-permute-done = bf16[32,2048]{1,0:T(8,128)(2,1)S(1)} collective-permute-done((bf16[32,2048]{1,0:T(8,128)(2,1)S(1)}, bf16[32,2048]{1,0:T(8,128)(2,1)S(1)}, u32[]{:S(2)}, u32[]{:S(2)}) %collective-permute-start) | collective-permute-done | bytes 131104 | tf_op jit(solution)/shard_map/while/body/eval_jaxpr/ppermute | solution.py:12
  219.4 1.5 fusion.35
  225.6 4.6 %collective-permute-done = bf16[32,2048]{1,0:T(8,128)(2,1)S(1)} collective-permute-done((bf16[32,2048]{1,0:T(8,128)(2,1)S(1)}, bf16[32,2048]{1,0:T(8,128)(2,1)S(1)}, u32[]{:S(2)}, u32[]{:S(2)}) %collective-permute-start) | collective-permute-done | bytes 131104 | tf_op jit(solution)/shard_map/while/body/eval_jaxpr/ppermute | solution.py:12
  230.8 1.5 fusion.35
  237.0 4.6 %collective-permute-done = bf16[32,2048]{1,0:T(8,128)(2,1)S(1)} collective-permute-done((bf16[32,2048]{1,0:T(8,128)(2,1)S(1)}, bf16[32,2048]{1,0:T(8,128)(2,1)S(1)}, u32[]{:S(2)}, u32[]{:S(2)}) %collective-permute-start) | collective-permute-done | bytes 131104 | tf_op jit(solution)/shard_map/while/body/eval_jaxpr/ppermute | solution.py:12
  242.2 1.5 fusion.35
  248.4 4.6 %collective-permute-done = bf16[32,2048]{1,0:T(8,128)(2,1)S(1)} collective-permute-done((bf16[32,2048]{1,0:T(8,128)(2,1)S(1)}, bf16[32,2048]{1,0:T(8,128)(2,1)S(1)}, u32[]{:S(2)}, u32[]{:S(2)}) %collective-permute-start) | collective-permute-done | bytes 131104 | tf_op jit(solution)/shard_map/while/body/eval_jaxpr/ppermute | solution.py:12
  253.6 1.5 fusion.35
  259.8 4.6 %collective-permute-done = bf16[32,2048]{1,0:T(8,128)(2,1)S(1)} collective-permute-done((bf16[32,2048]{1,0:T(8,128)(2,1)S(1)}, bf16[32,2048]{1,0:T(8,128)(2,1)S(1)}, u32[]{:S(2)}, u32[]{:S(2)}) %collective-permute-start) | collective-permute-done | bytes 131104 | tf_op jit(solution)/shard_map/while/body/eval_jaxpr/ppermute | solution.py:12
  265.0 1.5 fusion.35
  271.2 4.6 %collective-permute-done = bf16[32,2048]{1,0:T(8,128)(2,1)S(1)} collective-permute-done((bf16[32,2048]{1,0:T(8,128)(2,1)S(1)}, bf16[32,2048]{1,0:T(8,128)(2,1)S(1)}, u32[]{:S(2)}, u32[]{:S(2)}) %collective-permute-start) | collective-permute-done | bytes 131104 | tf_op jit(solution)/shard_map/while/body/eval_jaxpr/ppermute | solution.py:12
  276.4 1.5 fusion.35
  282.6 4.6 %collective-permute-done = bf16[32,2048]{1,0:T(8,128)(2,1)S(1)} collective-permute-done((bf16[32,2048]{1,0:T(8,128)(2,1)S(1)}, bf16[32,2048]{1,0:T(8,128)(2,1)S(1)}, u32[]{:S(2)}, u32[]{:S(2)}) %collective-permute-start) | collective-permute-done | bytes 131104 | tf_op jit(solution)/shard_map/while/body/eval_jaxpr/ppermute | solution.py:12
  287.8 1.5 fusion.35
  294.0 4.6 %collective-permute-done = bf16[32,2048]{1,0:T(8,128)(2,1)S(1)} collective-permute-done((bf16[32,2048]{1,0:T(8,128)(2,1)S(1)}, bf16[32,2048]{1,0:T(8,128)(2,1)S(1)}, u32[]{:S(2)}, u32[]{:S(2)}) %collective-permute-start) | collective-permute-done | bytes 131104 | tf_op jit(solution)/shard_map/while/body/eval_jaxpr/ppermute | solution.py:12
  299.2 1.5 fusion.35
  305.5 4.6 %collective-permute-done = bf16[32,2048]{1,0:T(8,128)(2,1)S(1)} collective-permute-done((bf16[32,2048]{1,0:T(8,128)(2,1)S(1)}, bf16[32,2048]{1,0:T(8,128)(2,1)S(1)}, u32[]{:S(2)}, u32[]{:S(2)}) %collective-permute-start) | collective-permute-done | bytes 131104 | tf_op jit(solution)/shard_map/while/body/eval_jaxpr/ppermute | solution.py:12
  310.6 1.5 fusion.35
  316.9 4.6 %collective-permute-done = bf16[32,2048]{1,0:T(8,128)(2,1)S(1)} collective-permute-done((bf16[32,2048]{1,0:T(8,128)(2,1)S(1)}, bf16[32,2048]{1,0:T(8,128)(2,1)S(1)}, u32[]{:S(2)}, u32[]{:S(2)}) %collective-permute-start) | collective-permute-done | bytes 131104 | tf_op jit(solution)/shard_map/while/body/eval_jaxpr/ppermute | solution.py:12
  322.0 1.5 fusion.35
  328.3 4.6 %collective-permute-done = bf16[32,2048]{1,0:T(8,128)(2,1)S(1)} collective-permute-done((bf16[32,2048]{1,0:T(8,128)(2,1)S(1)}, bf16[32,2048]{1,0:T(8,128)(2,1)S(1)}, u32[]{:S(2)}, u32[]{:S(2)}) %collective-permute-start) | collective-permute-done | bytes 131104 | tf_op jit(solution)/shard_map/while/body/eval_jaxpr/ppermute | solution.py:12
  333.4 1.5 fusion.35
  339.7 4.6 %collective-permute-done = bf16[32,2048]{1,0:T(8,128)(2,1)S(1)} collective-permute-done((bf16[32,2048]{1,0:T(8,128)(2,1)S(1)}, bf16[32,2048]{1,0:T(8,128)(2,1)S(1)}, u32[]{:S(2)}, u32[]{:S(2)}) %collective-permute-start) | collective-permute-done | bytes 131104 | tf_op jit(solution)/shard_map/while/body/eval_jaxpr/ppermute | solution.py:12
  344.8 1.5 fusion.35
  351.1 4.6 %collective-permute-done = bf16[32,2048]{1,0:T(8,128)(2,1)S(1)} collective-permute-done((bf16[32,2048]{1,0:T(8,128)(2,1)S(1)}, bf16[32,2048]{1,0:T(8,128)(2,1)S(1)}, u32[]{:S(2)}, u32[]{:S(2)}) %collective-permute-start) | collective-permute-done | bytes 131104 | tf_op jit(solution)/shard_map/while/body/eval_jaxpr/ppermute | solution.py:12
  359.7 52.2 %all-gather.2.cloned.1.call-done = bf16[256,2048]{1,0:T(8,128)(2,1)} async-done(((bf16[32,2048]{1,0:T(8,128)(2,1)}), bf16[256,2048]{1,0:T(8,128)(2,1)}) %all-gather.2.cloned.1.call-update) | async-done | bytes 1048592 | tf_op jit(solution)/shard_map/all_gather | solution.py:63
  411.9 2.3 fusion.11
  (359 shorter events, 161.1 us)
Async XLA Ops:
  6.5 405.3 %copy-start = (bf16[256,256]{1,0:T(8,128)(2,1)S(1)}, bf16[256,256]{1,0:T(8,128)(2,1)}, u32[]{:S(2)}) copy-start(bf16[256,256]{1,0:T(8,128)(2,1)} %param.15) | copy-start | bytes 393220
  6.5 405.3 %all-gather.2.cloned.1.call-start = ((), (), s32[]{:S(2)}) async-start(), calls=%async_computation | async-start | bytes 1179648 | tf_op jit(solution)/shard_map/all_gather | solution.py:63
  15.0 6.0 %collective-permute-start = (bf16[32,2048]{1,0:T(8,128)(2,1)S(1)}, bf16[32,2048]{1,0:T(8,128)(2,1)S(1)}, u32[]{:S(2)}, u32[]{:S(2)}) collective-permute-start(bf16[32,2048]{1,0:T(8,128)(2,1)S(1)} %get-tuple-element.350), channel_id=1, source_target_pairs={{248,0},{0,8},{8,16},{16,24},{24,32},{32,40},{40,48},{48,56},{56,6... | collective-permute-start | bytes 393224 | tf_op jit(solution)/shard_map/while/body/eval_jaxpr/ppermute | solution.py:12
  24.3 6.0 %collective-permute-start = (bf16[32,2048]{1,0:T(8,128)(2,1)S(1)}, bf16[32,2048]{1,0:T(8,128)(2,1)S(1)}, u32[]{:S(2)}, u32[]{:S(2)}) collective-permute-start(bf16[32,2048]{1,0:T(8,128)(2,1)S(1)} %get-tuple-element.350), channel_id=1, source_target_pairs={{248,0},{0,8},{8,16},{16,24},{24,32},{32,40},{40,48},{48,56},{56,6... | collective-permute-start | bytes 393224 | tf_op jit(solution)/shard_map/while/body/eval_jaxpr/ppermute | solution.py:12
  33.6 6.0 %collective-permute-start = (bf16[32,2048]{1,0:T(8,128)(2,1)S(1)}, bf16[32,2048]{1,0:T(8,128)(2,1)S(1)}, u32[]{:S(2)}, u32[]{:S(2)}) collective-permute-start(bf16[32,2048]{1,0:T(8,128)(2,1)S(1)} %get-tuple-element.350), channel_id=1, source_target_pairs={{248,0},{0,8},{8,16},{16,24},{24,32},{32,40},{40,48},{48,56},{56,6... | collective-permute-start | bytes 393224 | tf_op jit(solution)/shard_map/while/body/eval_jaxpr/ppermute | solution.py:12
  42.9 6.0 %collective-permute-start = (bf16[32,2048]{1,0:T(8,128)(2,1)S(1)}, bf16[32,2048]{1,0:T(8,128)(2,1)S(1)}, u32[]{:S(2)}, u32[]{:S(2)}) collective-permute-start(bf16[32,2048]{1,0:T(8,128)(2,1)S(1)} %get-tuple-element.350), channel_id=1, source_target_pairs={{248,0},{0,8},{8,16},{16,24},{24,32},{32,40},{40,48},{48,56},{56,6... | collective-permute-start | bytes 393224 | tf_op jit(solution)/shard_map/while/body/eval_jaxpr/ppermute | solution.py:12
  52.2 7.0 %collective-permute-start = (bf16[32,2048]{1,0:T(8,128)(2,1)S(1)}, bf16[32,2048]{1,0:T(8,128)(2,1)S(1)}, u32[]{:S(2)}, u32[]{:S(2)}) collective-permute-start(bf16[32,2048]{1,0:T(8,128)(2,1)S(1)} %get-tuple-element.350), channel_id=1, source_target_pairs={{248,0},{0,8},{8,16},{16,24},{24,32},{32,40},{40,48},{48,56},{56,6... | collective-permute-start | bytes 393224 | tf_op jit(solution)/shard_map/while/body/eval_jaxpr/ppermute | solution.py:12
  62.5 8.1 %collective-permute-start = (bf16[32,2048]{1,0:T(8,128)(2,1)S(1)}, bf16[32,2048]{1,0:T(8,128)(2,1)S(1)}, u32[]{:S(2)}, u32[]{:S(2)}) collective-permute-start(bf16[32,2048]{1,0:T(8,128)(2,1)S(1)} %get-tuple-element.350), channel_id=1, source_target_pairs={{248,0},{0,8},{8,16},{16,24},{24,32},{32,40},{40,48},{48,56},{56,6... | collective-permute-start | bytes 393224 | tf_op jit(solution)/shard_map/while/body/eval_jaxpr/ppermute | solution.py:12
  73.9 8.1 %collective-permute-start = (bf16[32,2048]{1,0:T(8,128)(2,1)S(1)}, bf16[32,2048]{1,0:T(8,128)(2,1)S(1)}, u32[]{:S(2)}, u32[]{:S(2)}) collective-permute-start(bf16[32,2048]{1,0:T(8,128)(2,1)S(1)} %get-tuple-element.350), channel_id=1, source_target_pairs={{248,0},{0,8},{8,16},{16,24},{24,32},{32,40},{40,48},{48,56},{56,6... | collective-permute-start | bytes 393224 | tf_op jit(solution)/shard_map/while/body/eval_jaxpr/ppermute | solution.py:12
  85.3 8.1 %collective-permute-start = (bf16[32,2048]{1,0:T(8,128)(2,1)S(1)}, bf16[32,2048]{1,0:T(8,128)(2,1)S(1)}, u32[]{:S(2)}, u32[]{:S(2)}) collective-permute-start(bf16[32,2048]{1,0:T(8,128)(2,1)S(1)} %get-tuple-element.350), channel_id=1, source_target_pairs={{248,0},{0,8},{8,16},{16,24},{24,32},{32,40},{40,48},{48,56},{56,6... | collective-permute-start | bytes 393224 | tf_op jit(solution)/shard_map/while/body/eval_jaxpr/ppermute | solution.py:12
  96.7 8.1 %collective-permute-start = (bf16[32,2048]{1,0:T(8,128)(2,1)S(1)}, bf16[32,2048]{1,0:T(8,128)(2,1)S(1)}, u32[]{:S(2)}, u32[]{:S(2)}) collective-permute-start(bf16[32,2048]{1,0:T(8,128)(2,1)S(1)} %get-tuple-element.350), channel_id=1, source_target_pairs={{248,0},{0,8},{8,16},{16,24},{24,32},{32,40},{40,48},{48,56},{56,6... | collective-permute-start | bytes 393224 | tf_op jit(solution)/shard_map/while/body/eval_jaxpr/ppermute | solution.py:12
  108.1 8.1 %collective-permute-start = (bf16[32,2048]{1,0:T(8,128)(2,1)S(1)}, bf16[32,2048]{1,0:T(8,128)(2,1)S(1)}, u32[]{:S(2)}, u32[]{:S(2)}) collective-permute-start(bf16[32,2048]{1,0:T(8,128)(2,1)S(1)} %get-tuple-element.350), channel_id=1, source_target_pairs={{248,0},{0,8},{8,16},{16,24},{24,32},{32,40},{40,48},{48,56},{56,6... | collective-permute-start | bytes 393224 | tf_op jit(solution)/shard_map/while/body/eval_jaxpr/ppermute | solution.py:12
  119.5 8.1 %collective-permute-start = (bf16[32,2048]{1,0:T(8,128)(2,1)S(1)}, bf16[32,2048]{1,0:T(8,128)(2,1)S(1)}, u32[]{:S(2)}, u32[]{:S(2)}) collective-permute-start(bf16[32,2048]{1,0:T(8,128)(2,1)S(1)} %get-tuple-element.350), channel_id=1, source_target_pairs={{248,0},{0,8},{8,16},{16,24},{24,32},{32,40},{40,48},{48,56},{56,6... | collective-permute-start | bytes 393224 | tf_op jit(solution)/shard_map/while/body/eval_jaxpr/ppermute | solution.py:12
  130.9 8.1 %collective-permute-start = (bf16[32,2048]{1,0:T(8,128)(2,1)S(1)}, bf16[32,2048]{1,0:T(8,128)(2,1)S(1)}, u32[]{:S(2)}, u32[]{:S(2)}) collective-permute-start(bf16[32,2048]{1,0:T(8,128)(2,1)S(1)} %get-tuple-element.350), channel_id=1, source_target_pairs={{248,0},{0,8},{8,16},{16,24},{24,32},{32,40},{40,48},{48,56},{56,6... | collective-permute-start | bytes 393224 | tf_op jit(solution)/shard_map/while/body/eval_jaxpr/ppermute | solution.py:12
  142.3 8.1 %collective-permute-start = (bf16[32,2048]{1,0:T(8,128)(2,1)S(1)}, bf16[32,2048]{1,0:T(8,128)(2,1)S(1)}, u32[]{:S(2)}, u32[]{:S(2)}) collective-permute-start(bf16[32,2048]{1,0:T(8,128)(2,1)S(1)} %get-tuple-element.350), channel_id=1, source_target_pairs={{248,0},{0,8},{8,16},{16,24},{24,32},{32,40},{40,48},{48,56},{56,6... | collective-permute-start | bytes 393224 | tf_op jit(solution)/shard_map/while/body/eval_jaxpr/ppermute | solution.py:12
  153.7 8.1 %collective-permute-start = (bf16[32,2048]{1,0:T(8,128)(2,1)S(1)}, bf16[32,2048]{1,0:T(8,128)(2,1)S(1)}, u32[]{:S(2)}, u32[]{:S(2)}) collective-permute-start(bf16[32,2048]{1,0:T(8,128)(2,1)S(1)} %get-tuple-element.350), channel_id=1, source_target_pairs={{248,0},{0,8},{8,16},{16,24},{24,32},{32,40},{40,48},{48,56},{56,6... | collective-permute-start | bytes 393224 | tf_op jit(solution)/shard_map/while/body/eval_jaxpr/ppermute | solution.py:12
  165.1 8.1 %collective-permute-start = (bf16[32,2048]{1,0:T(8,128)(2,1)S(1)}, bf16[32,2048]{1,0:T(8,128)(2,1)S(1)}, u32[]{:S(2)}, u32[]{:S(2)}) collective-permute-start(bf16[32,2048]{1,0:T(8,128)(2,1)S(1)} %get-tuple-element.350), channel_id=1, source_target_pairs={{248,0},{0,8},{8,16},{16,24},{24,32},{32,40},{40,48},{48,56},{56,6... | collective-permute-start | bytes 393224 | tf_op jit(solution)/shard_map/while/body/eval_jaxpr/ppermute | solution.py:12
  176.5 8.1 %collective-permute-start = (bf16[32,2048]{1,0:T(8,128)(2,1)S(1)}, bf16[32,2048]{1,0:T(8,128)(2,1)S(1)}, u32[]{:S(2)}, u32[]{:S(2)}) collective-permute-start(bf16[32,2048]{1,0:T(8,128)(2,1)S(1)} %get-tuple-element.350), channel_id=1, source_target_pairs={{248,0},{0,8},{8,16},{16,24},{24,32},{32,40},{40,48},{48,56},{56,6... | collective-permute-start | bytes 393224 | tf_op jit(solution)/shard_map/while/body/eval_jaxpr/ppermute | solution.py:12
  187.9 8.1 %collective-permute-start = (bf16[32,2048]{1,0:T(8,128)(2,1)S(1)}, bf16[32,2048]{1,0:T(8,128)(2,1)S(1)}, u32[]{:S(2)}, u32[]{:S(2)}) collective-permute-start(bf16[32,2048]{1,0:T(8,128)(2,1)S(1)} %get-tuple-element.350), channel_id=1, source_target_pairs={{248,0},{0,8},{8,16},{16,24},{24,32},{32,40},{40,48},{48,56},{56,6... | collective-permute-start | bytes 393224 | tf_op jit(solution)/shard_map/while/body/eval_jaxpr/ppermute | solution.py:12
  199.3 8.1 %collective-permute-start = (bf16[32,2048]{1,0:T(8,128)(2,1)S(1)}, bf16[32,2048]{1,0:T(8,128)(2,1)S(1)}, u32[]{:S(2)}, u32[]{:S(2)}) collective-permute-start(bf16[32,2048]{1,0:T(8,128)(2,1)S(1)} %get-tuple-element.350), channel_id=1, source_target_pairs={{248,0},{0,8},{8,16},{16,24},{24,32},{32,40},{40,48},{48,56},{56,6... | collective-permute-start | bytes 393224 | tf_op jit(solution)/shard_map/while/body/eval_jaxpr/ppermute | solution.py:12
  210.7 8.1 %collective-permute-start = (bf16[32,2048]{1,0:T(8,128)(2,1)S(1)}, bf16[32,2048]{1,0:T(8,128)(2,1)S(1)}, u32[]{:S(2)}, u32[]{:S(2)}) collective-permute-start(bf16[32,2048]{1,0:T(8,128)(2,1)S(1)} %get-tuple-element.350), channel_id=1, source_target_pairs={{248,0},{0,8},{8,16},{16,24},{24,32},{32,40},{40,48},{48,56},{56,6... | collective-permute-start | bytes 393224 | tf_op jit(solution)/shard_map/while/body/eval_jaxpr/ppermute | solution.py:12
  222.1 8.1 %collective-permute-start = (bf16[32,2048]{1,0:T(8,128)(2,1)S(1)}, bf16[32,2048]{1,0:T(8,128)(2,1)S(1)}, u32[]{:S(2)}, u32[]{:S(2)}) collective-permute-start(bf16[32,2048]{1,0:T(8,128)(2,1)S(1)} %get-tuple-element.350), channel_id=1, source_target_pairs={{248,0},{0,8},{8,16},{16,24},{24,32},{32,40},{40,48},{48,56},{56,6... | collective-permute-start | bytes 393224 | tf_op jit(solution)/shard_map/while/body/eval_jaxpr/ppermute | solution.py:12
  233.5 8.1 %collective-permute-start = (bf16[32,2048]{1,0:T(8,128)(2,1)S(1)}, bf16[32,2048]{1,0:T(8,128)(2,1)S(1)}, u32[]{:S(2)}, u32[]{:S(2)}) collective-permute-start(bf16[32,2048]{1,0:T(8,128)(2,1)S(1)} %get-tuple-element.350), channel_id=1, source_target_pairs={{248,0},{0,8},{8,16},{16,24},{24,32},{32,40},{40,48},{48,56},{56,6... | collective-permute-start | bytes 393224 | tf_op jit(solution)/shard_map/while/body/eval_jaxpr/ppermute | solution.py:12
  244.9 8.1 %collective-permute-start = (bf16[32,2048]{1,0:T(8,128)(2,1)S(1)}, bf16[32,2048]{1,0:T(8,128)(2,1)S(1)}, u32[]{:S(2)}, u32[]{:S(2)}) collective-permute-start(bf16[32,2048]{1,0:T(8,128)(2,1)S(1)} %get-tuple-element.350), channel_id=1, source_target_pairs={{248,0},{0,8},{8,16},{16,24},{24,32},{32,40},{40,48},{48,56},{56,6... | collective-permute-start | bytes 393224 | tf_op jit(solution)/shard_map/while/body/eval_jaxpr/ppermute | solution.py:12
  256.3 8.1 %collective-permute-start = (bf16[32,2048]{1,0:T(8,128)(2,1)S(1)}, bf16[32,2048]{1,0:T(8,128)(2,1)S(1)}, u32[]{:S(2)}, u32[]{:S(2)}) collective-permute-start(bf16[32,2048]{1,0:T(8,128)(2,1)S(1)} %get-tuple-element.350), channel_id=1, source_target_pairs={{248,0},{0,8},{8,16},{16,24},{24,32},{32,40},{40,48},{48,56},{56,6... | collective-permute-start | bytes 393224 | tf_op jit(solution)/shard_map/while/body/eval_jaxpr/ppermute | solution.py:12
  267.7 8.1 %collective-permute-start = (bf16[32,2048]{1,0:T(8,128)(2,1)S(1)}, bf16[32,2048]{1,0:T(8,128)(2,1)S(1)}, u32[]{:S(2)}, u32[]{:S(2)}) collective-permute-start(bf16[32,2048]{1,0:T(8,128)(2,1)S(1)} %get-tuple-element.350), channel_id=1, source_target_pairs={{248,0},{0,8},{8,16},{16,24},{24,32},{32,40},{40,48},{48,56},{56,6... | collective-permute-start | bytes 393224 | tf_op jit(solution)/shard_map/while/body/eval_jaxpr/ppermute | solution.py:12
  279.1 8.1 %collective-permute-start = (bf16[32,2048]{1,0:T(8,128)(2,1)S(1)}, bf16[32,2048]{1,0:T(8,128)(2,1)S(1)}, u32[]{:S(2)}, u32[]{:S(2)}) collective-permute-start(bf16[32,2048]{1,0:T(8,128)(2,1)S(1)} %get-tuple-element.350), channel_id=1, source_target_pairs={{248,0},{0,8},{8,16},{16,24},{24,32},{32,40},{40,48},{48,56},{56,6... | collective-permute-start | bytes 393224 | tf_op jit(solution)/shard_map/while/body/eval_jaxpr/ppermute | solution.py:12
  290.5 8.1 %collective-permute-start = (bf16[32,2048]{1,0:T(8,128)(2,1)S(1)}, bf16[32,2048]{1,0:T(8,128)(2,1)S(1)}, u32[]{:S(2)}, u32[]{:S(2)}) collective-permute-start(bf16[32,2048]{1,0:T(8,128)(2,1)S(1)} %get-tuple-element.350), channel_id=1, source_target_pairs={{248,0},{0,8},{8,16},{16,24},{24,32},{32,40},{40,48},{48,56},{56,6... | collective-permute-start | bytes 393224 | tf_op jit(solution)/shard_map/while/body/eval_jaxpr/ppermute | solution.py:12
  301.9 8.1 %collective-permute-start = (bf16[32,2048]{1,0:T(8,128)(2,1)S(1)}, bf16[32,2048]{1,0:T(8,128)(2,1)S(1)}, u32[]{:S(2)}, u32[]{:S(2)}) collective-permute-start(bf16[32,2048]{1,0:T(8,128)(2,1)S(1)} %get-tuple-element.350), channel_id=1, source_target_pairs={{248,0},{0,8},{8,16},{16,24},{24,32},{32,40},{40,48},{48,56},{56,6... | collective-permute-start | bytes 393224 | tf_op jit(solution)/shard_map/while/body/eval_jaxpr/ppermute | solution.py:12
  313.3 8.1 %collective-permute-start = (bf16[32,2048]{1,0:T(8,128)(2,1)S(1)}, bf16[32,2048]{1,0:T(8,128)(2,1)S(1)}, u32[]{:S(2)}, u32[]{:S(2)}) collective-permute-start(bf16[32,2048]{1,0:T(8,128)(2,1)S(1)} %get-tuple-element.350), channel_id=1, source_target_pairs={{248,0},{0,8},{8,16},{16,24},{24,32},{32,40},{40,48},{48,56},{56,6... | collective-permute-start | bytes 393224 | tf_op jit(solution)/shard_map/while/body/eval_jaxpr/ppermute | solution.py:12
  324.7 8.1 %collective-permute-start = (bf16[32,2048]{1,0:T(8,128)(2,1)S(1)}, bf16[32,2048]{1,0:T(8,128)(2,1)S(1)}, u32[]{:S(2)}, u32[]{:S(2)}) collective-permute-start(bf16[32,2048]{1,0:T(8,128)(2,1)S(1)} %get-tuple-element.350), channel_id=1, source_target_pairs={{248,0},{0,8},{8,16},{16,24},{24,32},{32,40},{40,48},{48,56},{56,6... | collective-permute-start | bytes 393224 | tf_op jit(solution)/shard_map/while/body/eval_jaxpr/ppermute | solution.py:12
  336.2 8.1 %collective-permute-start = (bf16[32,2048]{1,0:T(8,128)(2,1)S(1)}, bf16[32,2048]{1,0:T(8,128)(2,1)S(1)}, u32[]{:S(2)}, u32[]{:S(2)}) collective-permute-start(bf16[32,2048]{1,0:T(8,128)(2,1)S(1)} %get-tuple-element.350), channel_id=1, source_target_pairs={{248,0},{0,8},{8,16},{16,24},{24,32},{32,40},{40,48},{48,56},{56,6... | collective-permute-start | bytes 393224 | tf_op jit(solution)/shard_map/while/body/eval_jaxpr/ppermute | solution.py:12
  347.6 8.1 %collective-permute-start = (bf16[32,2048]{1,0:T(8,128)(2,1)S(1)}, bf16[32,2048]{1,0:T(8,128)(2,1)S(1)}, u32[]{:S(2)}, u32[]{:S(2)}) collective-permute-start(bf16[32,2048]{1,0:T(8,128)(2,1)S(1)} %get-tuple-element.350), channel_id=1, source_target_pairs={{248,0},{0,8},{8,16},{16,24},{24,32},{32,40},{40,48},{48,56},{56,6... | collective-permute-start | bytes 393224 | tf_op jit(solution)/shard_map/while/body/eval_jaxpr/ppermute | solution.py:12
Sparse Core Ops, SparseCore 0:
  359.8 52.0 all-gather.1
where the time goes:
time: 424 us; the launch traced here: 421 us
  waiting for transfers between devices  178 us (42%)
  other arithmetic  130 us (31%)
  matrix products  49.1 us (12%)
  local copies, waits for them, and re-layouts  20.5 us (5%)
  loops' own time  19.7 us (5%)
  between operations  14.7 us (3%)
  starting transfers between devices  9.36 us (2%)
    ppermute x31, waiting for transfers between devices, shifted(): return lax.ppermute(block, axis, route)  125 us
    all_gather x1, waiting for transfers between devices, body(): lax.all_gather(rounded, 'feat', axis=0, tiled=True)  52.2 us
    dot_general x32, matrix products, add_tiles(): jnp.einsum('hwj,wij->hwi', picked, tile_group, preferred_element_type=jnp...  46.8 us
    reduce_sum x32, other arithmetic, add_slab(): before = jnp.sum(((source_slab < slab_index) & usable).astype(jnp.int32))  40.1 us
    scatter-add x32, other arithmetic, add_tiles(): return totals.at[:, target_blocks, :].add(masked)  38.7 us
    select_n x32, other arithmetic, add_tiles(): return totals.at[:, target_blocks, :].add(masked)  24.1 us
    and x32, other arithmetic, add_slab(): (source_slab == slab_index) & usable  20.8 us
    another operation x1, loops' own time, body(): lax.fori_loop(1, slab_count, forward_turn, (add_slab(zero_totals, feature...  19.7 us
  transfers between devices with their start and end apart: 32, of which 32 were waited for; matrix products, arithmetic and copies ran while one was open for 21% of the time, Pallas kernels for 0%

commit v1 on v0

--- a/solution.py
+++ b/solution.py
@@ -4,6 +4,11 @@
 from jax.sharding import PartitionSpec as P
 
 PAIR_MOST = 16
+
+
+def swapped_in(shard, axis, d):
+    sent = jnp.stack([shard] * lax.axis_size(axis))
+    return jnp.concatenate(lax.all_to_all(sent, axis, 0, 0), axis=d)
 
 
 def shifted(block, axis, distance):
@@ -58,10 +63,7 @@
         weight, lax.axis_index("feat") * feature_rows, feature_rows, 1
     )
     combined = jnp.einsum(
-        "ko,kn->on",
-        columns,
-        lax.all_gather(rounded, "feat", axis=0, tiled=True),
-        preferred_element_type=jnp.float32,
+        "ko,kn->on", columns, swapped_in(rounded, "feat", 0), preferred_element_type=jnp.float32
     )
     return jnp.maximum(combined, 0.0).astype(jnp.bfloat16)
 

time: 424 us -> 385 us (0.908)
  the two profiles are of different devices: /device:TPU:4 before, /device:TPU:2 now
where the time goes in v1:
time: 385 us; the launch traced here: 382 us
  waiting for transfers between devices  153 us (40%)
  other arithmetic  130 us (34%)
  matrix products  47.8 us (12%)
  local copies, waits for them, and re-layouts  21.6 us (6%)
  loops' own time  19.8 us (5%)
  starting transfers between devices  8.51 us (2%)
    ppermute x31, waiting for transfers between devices, shifted(): return lax.ppermute(block, axis, route)  143 us
    dot_general x32, matrix products, add_tiles(): jnp.einsum('hwj,wij->hwi', picked, tile_group, preferred_element_type=jnp...  46.8 us
    reduce_sum x32, other arithmetic, add_slab(): before = jnp.sum(((source_slab < slab_index) & usable).astype(jnp.int32))  40.1 us
    scatter-add x32, other arithmetic, add_tiles(): return totals.at[:, target_blocks, :].add(masked)  38.7 us
    select_n x32, other arithmetic, add_tiles(): return totals.at[:, target_blocks, :].add(masked)  24.1 us
    and x32, other arithmetic, add_slab(): (source_slab == slab_index) & usable  20.8 us
    another operation x1, loops' own time, body(): lax.fori_loop(1, slab_count, forward_turn, (add_slab(zero_totals, feature...  19.8 us
    gather x32, local copies, waits for them, and re-layouts, add_tiles(): picked = jnp.take(blocks, source_blocks, axis=1)  18.4 us
  transfers between devices with their start and end apart: 32, of which 32 were waited for; matrix products, arithmetic and copies ran while one was open for 23% of the time, Pallas kernels for 0%

profile of v1, /device:TPU:2, one launch (start us, length us, event | category | flops | bytes accessed | tf_op | source)
XLA Modules:
  0.0 381.7 jit_solution(12770760089464473410)
XLA Ops:
  8.4 355.1 %while.18 = (s32[]{:T(128)}, f32[32,16,128]{2,0,1:T(8,128)S(1)}, bf16[32,2048]{1,0:T(8,128)(2,1)S(1)}, s32[]{:T(128)}, s32[256]{0:T(256)S(1)}, /*index=5*/s32[25...) while((s32[]{:T(128)}, f32[32,16,128]{2,0,1:T(8,128)S(1)}, ...), condition=%wide.region_5.7_spmd.clone, body=%wide.region_2.6_spmd.clone.sunk | while | flops 16977072 | bytes 3022064 | solution.py:58
  12.0 6.1 %collective-permute-done = bf16[32,2048]{1,0:T(8,128)(2,1)S(1)} collective-permute-done((bf16[32,2048]{1,0:T(8,128)(2,1)S(1)}, bf16[32,2048]{1,0:T(8,128)(2,1)S(1)}, u32[]{:S(2)}, u32[]{:S(2)}) %collective-permute-start) | collective-permute-done | bytes 131104 | tf_op jit(solution)/shard_map/while/body/eval_jaxpr/ppermute | solution.py:17
  18.6 1.5 fusion.35
  24.9 4.6 %collective-permute-done = bf16[32,2048]{1,0:T(8,128)(2,1)S(1)} collective-permute-done((bf16[32,2048]{1,0:T(8,128)(2,1)S(1)}, bf16[32,2048]{1,0:T(8,128)(2,1)S(1)}, u32[]{:S(2)}, u32[]{:S(2)}) %collective-permute-start) | collective-permute-done | bytes 131104 | tf_op jit(solution)/shard_map/while/body/eval_jaxpr/ppermute | solution.py:17
  30.0 1.5 fusion.35
  36.3 4.6 %collective-permute-done = bf16[32,2048]{1,0:T(8,128)(2,1)S(1)} collective-permute-done((bf16[32,2048]{1,0:T(8,128)(2,1)S(1)}, bf16[32,2048]{1,0:T(8,128)(2,1)S(1)}, u32[]{:S(2)}, u32[]{:S(2)}) %collective-permute-start) | collective-permute-done | bytes 131104 | tf_op jit(solution)/shard_map/while/body/eval_jaxpr/ppermute | solution.py:17
  41.4 1.5 fusion.35
  47.7 4.6 %collective-permute-done = bf16[32,2048]{1,0:T(8,128)(2,1)S(1)} collective-permute-done((bf16[32,2048]{1,0:T(8,128)(2,1)S(1)}, bf16[32,2048]{1,0:T(8,128)(2,1)S(1)}, u32[]{:S(2)}, u32[]{:S(2)}) %collective-permute-start) | collective-permute-done | bytes 131104 | tf_op jit(solution)/shard_map/while/body/eval_jaxpr/ppermute | solution.py:17
  52.8 1.5 fusion.35
  59.1 4.6 %collective-permute-done = bf16[32,2048]{1,0:T(8,128)(2,1)S(1)} collective-permute-done((bf16[32,2048]{1,0:T(8,128)(2,1)S(1)}, bf16[32,2048]{1,0:T(8,128)(2,1)S(1)}, u32[]{:S(2)}, u32[]{:S(2)}) %collective-permute-start) | collective-permute-done | bytes 131104 | tf_op jit(solution)/shard_map/while/body/eval_jaxpr/ppermute | solution.py:17
  64.2 1.5 fusion.35
  70.5 4.6 %collective-permute-done = bf16[32,2048]{1,0:T(8,128)(2,1)S(1)} collective-permute-done((bf16[32,2048]{1,0:T(8,128)(2,1)S(1)}, bf16[32,2048]{1,0:T(8,128)(2,1)S(1)}, u32[]{:S(2)}, u32[]{:S(2)}) %collective-permute-start) | collective-permute-done | bytes 131104 | tf_op jit(solution)/shard_map/while/body/eval_jaxpr/ppermute | solution.py:17
  75.6 1.5 fusion.35
  81.9 4.6 %collective-permute-done = bf16[32,2048]{1,0:T(8,128)(2,1)S(1)} collective-permute-done((bf16[32,2048]{1,0:T(8,128)(2,1)S(1)}, bf16[32,2048]{1,0:T(8,128)(2,1)S(1)}, u32[]{:S(2)}, u32[]{:S(2)}) %collective-permute-start) | collective-permute-done | bytes 131104 | tf_op jit(solution)/shard_map/while/body/eval_jaxpr/ppermute | solution.py:17
  87.0 1.5 fusion.35
  93.3 4.6 %collective-permute-done = bf16[32,2048]{1,0:T(8,128)(2,1)S(1)} collective-permute-done((bf16[32,2048]{1,0:T(8,128)(2,1)S(1)}, bf16[32,2048]{1,0:T(8,128)(2,1)S(1)}, u32[]{:S(2)}, u32[]{:S(2)}) %collective-permute-start) | collective-permute-done | bytes 131104 | tf_op jit(solution)/shard_map/while/body/eval_jaxpr/ppermute | solution.py:17
  98.4 1.5 fusion.35
  104.7 4.6 %collective-permute-done = bf16[32,2048]{1,0:T(8,128)(2,1)S(1)} collective-permute-done((bf16[32,2048]{1,0:T(8,128)(2,1)S(1)}, bf16[32,2048]{1,0:T(8,128)(2,1)S(1)}, u32[]{:S(2)}, u32[]{:S(2)}) %collective-permute-start) | collective-permute-done | bytes 131104 | tf_op jit(solution)/shard_map/while/body/eval_jaxpr/ppermute | solution.py:17
  109.8 1.5 fusion.35
  116.1 4.6 %collective-permute-done = bf16[32,2048]{1,0:T(8,128)(2,1)S(1)} collective-permute-done((bf16[32,2048]{1,0:T(8,128)(2,1)S(1)}, bf16[32,2048]{1,0:T(8,128)(2,1)S(1)}, u32[]{:S(2)}, u32[]{:S(2)}) %collective-permute-start) | collective-permute-done | bytes 131104 | tf_op jit(solution)/shard_map/while/body/eval_jaxpr/ppermute | solution.py:17
  121.2 1.5 fusion.35
  127.5 4.6 %collective-permute-done = bf16[32,2048]{1,0:T(8,128)(2,1)S(1)} collective-permute-done((bf16[32,2048]{1,0:T(8,128)(2,1)S(1)}, bf16[32,2048]{1,0:T(8,128)(2,1)S(1)}, u32[]{:S(2)}, u32[]{:S(2)}) %collective-permute-start) | collective-permute-done | bytes 131104 | tf_op jit(solution)/shard_map/while/body/eval_jaxpr/ppermute | solution.py:17
  132.6 1.5 fusion.35
  138.9 4.6 %collective-permute-done = bf16[32,2048]{1,0:T(8,128)(2,1)S(1)} collective-permute-done((bf16[32,2048]{1,0:T(8,128)(2,1)S(1)}, bf16[32,2048]{1,0:T(8,128)(2,1)S(1)}, u32[]{:S(2)}, u32[]{:S(2)}) %collective-permute-start) | collective-permute-done | bytes 131104 | tf_op jit(solution)/shard_map/while/body/eval_jaxpr/ppermute | solution.py:17
  144.0 1.5 fusion.35
  150.3 4.6 %collective-permute-done = bf16[32,2048]{1,0:T(8,128)(2,1)S(1)} collective-permute-done((bf16[32,2048]{1,0:T(8,128)(2,1)S(1)}, bf16[32,2048]{1,0:T(8,128)(2,1)S(1)}, u32[]{:S(2)}, u32[]{:S(2)}) %collective-permute-start) | collective-permute-done | bytes 131104 | tf_op jit(solution)/shard_map/while/body/eval_jaxpr/ppermute | solution.py:17
  155.4 1.5 fusion.35
  161.7 4.6 %collective-permute-done = bf16[32,2048]{1,0:T(8,128)(2,1)S(1)} collective-permute-done((bf16[32,2048]{1,0:T(8,128)(2,1)S(1)}, bf16[32,2048]{1,0:T(8,128)(2,1)S(1)}, u32[]{:S(2)}, u32[]{:S(2)}) %collective-permute-start) | collective-permute-done | bytes 131104 | tf_op jit(solution)/shard_map/while/body/eval_jaxpr/ppermute | solution.py:17
  166.8 1.5 fusion.35
  173.1 4.6 %collective-permute-done = bf16[32,2048]{1,0:T(8,128)(2,1)S(1)} collective-permute-done((bf16[32,2048]{1,0:T(8,128)(2,1)S(1)}, bf16[32,2048]{1,0:T(8,128)(2,1)S(1)}, u32[]{:S(2)}, u32[]{:S(2)}) %collective-permute-start) | collective-permute-done | bytes 131104 | tf_op jit(solution)/shard_map/while/body/eval_jaxpr/ppermute | solution.py:17
  178.2 1.5 fusion.35
  184.5 4.6 %collective-permute-done = bf16[32,2048]{1,0:T(8,128)(2,1)S(1)} collective-permute-done((bf16[32,2048]{1,0:T(8,128)(2,1)S(1)}, bf16[32,2048]{1,0:T(8,128)(2,1)S(1)}, u32[]{:S(2)}, u32[]{:S(2)}) %collective-permute-start) | collective-permute-done | bytes 131104 | tf_op jit(solution)/shard_map/while/body/eval_jaxpr/ppermute | solution.py:17
  189.6 1.5 fusion.35
  195.9 4.6 %collective-permute-done = bf16[32,2048]{1,0:T(8,128)(2,1)S(1)} collective-permute-done((bf16[32,2048]{1,0:T(8,128)(2,1)S(1)}, bf16[32,2048]{1,0:T(8,128)(2,1)S(1)}, u32[]{:S(2)}, u32[]{:S(2)}) %collective-permute-start) | collective-permute-done | bytes 131104 | tf_op jit(solution)/shard_map/while/body/eval_jaxpr/ppermute | solution.py:17
  201.0 1.5 fusion.35
  207.3 4.6 %collective-permute-done = bf16[32,2048]{1,0:T(8,128)(2,1)S(1)} collective-permute-done((bf16[32,2048]{1,0:T(8,128)(2,1)S(1)}, bf16[32,2048]{1,0:T(8,128)(2,1)S(1)}, u32[]{:S(2)}, u32[]{:S(2)}) %collective-permute-start) | collective-permute-done | bytes 131104 | tf_op jit(solution)/shard_map/while/body/eval_jaxpr/ppermute | solution.py:17
  212.4 1.5 fusion.35
  218.7 4.6 %collective-permute-done = bf16[32,2048]{1,0:T(8,128)(2,1)S(1)} collective-permute-done((bf16[32,2048]{1,0:T(8,128)(2,1)S(1)}, bf16[32,2048]{1,0:T(8,128)(2,1)S(1)}, u32[]{:S(2)}, u32[]{:S(2)}) %collective-permute-start) | collective-permute-done | bytes 131104 | tf_op jit(solution)/shard_map/while/body/eval_jaxpr/ppermute | solution.py:17
  223.8 1.5 fusion.35
  230.1 4.6 %collective-permute-done = bf16[32,2048]{1,0:T(8,128)(2,1)S(1)} collective-permute-done((bf16[32,2048]{1,0:T(8,128)(2,1)S(1)}, bf16[32,2048]{1,0:T(8,128)(2,1)S(1)}, u32[]{:S(2)}, u32[]{:S(2)}) %collective-permute-start) | collective-permute-done | bytes 131104 | tf_op jit(solution)/shard_map/while/body/eval_jaxpr/ppermute | solution.py:17
  235.2 1.5 fusion.35
  241.5 4.6 %collective-permute-done = bf16[32,2048]{1,0:T(8,128)(2,1)S(1)} collective-permute-done((bf16[32,2048]{1,0:T(8,128)(2,1)S(1)}, bf16[32,2048]{1,0:T(8,128)(2,1)S(1)}, u32[]{:S(2)}, u32[]{:S(2)}) %collective-permute-start) | collective-permute-done | bytes 131104 | tf_op jit(solution)/shard_map/while/body/eval_jaxpr/ppermute | solution.py:17
  246.7 1.5 fusion.35
  252.9 4.6 %collective-permute-done = bf16[32,2048]{1,0:T(8,128)(2,1)S(1)} collective-permute-done((bf16[32,2048]{1,0:T(8,128)(2,1)S(1)}, bf16[32,2048]{1,0:T(8,128)(2,1)S(1)}, u32[]{:S(2)}, u32[]{:S(2)}) %collective-permute-start) | collective-permute-done | bytes 131104 | tf_op jit(solution)/shard_map/while/body/eval_jaxpr/ppermute | solution.py:17
  258.1 1.5 fusion.35
  264.3 4.6 %collective-permute-done = bf16[32,2048]{1,0:T(8,128)(2,1)S(1)} collective-permute-done((bf16[32,2048]{1,0:T(8,128)(2,1)S(1)}, bf16[32,2048]{1,0:T(8,128)(2,1)S(1)}, u32[]{:S(2)}, u32[]{:S(2)}) %collective-permute-start) | collective-permute-done | bytes 131104 | tf_op jit(solution)/shard_map/while/body/eval_jaxpr/ppermute | solution.py:17
  269.5 1.5 fusion.35
  275.7 4.6 %collective-permute-done = bf16[32,2048]{1,0:T(8,128)(2,1)S(1)} collective-permute-done((bf16[32,2048]{1,0:T(8,128)(2,1)S(1)}, bf16[32,2048]{1,0:T(8,128)(2,1)S(1)}, u32[]{:S(2)}, u32[]{:S(2)}) %collective-permute-start) | collective-permute-done | bytes 131104 | tf_op jit(solution)/shard_map/while/body/eval_jaxpr/ppermute | solution.py:17
  280.9 1.5 fusion.35
  287.1 4.6 %collective-permute-done = bf16[32,2048]{1,0:T(8,128)(2,1)S(1)} collective-permute-done((bf16[32,2048]{1,0:T(8,128)(2,1)S(1)}, bf16[32,2048]{1,0:T(8,128)(2,1)S(1)}, u32[]{:S(2)}, u32[]{:S(2)}) %collective-permute-start) | collective-permute-done | bytes 131104 | tf_op jit(solution)/shard_map/while/body/eval_jaxpr/ppermute | solution.py:17
  292.3 1.5 fusion.35
  298.5 4.6 %collective-permute-done = bf16[32,2048]{1,0:T(8,128)(2,1)S(1)} collective-permute-done((bf16[32,2048]{1,0:T(8,128)(2,1)S(1)}, bf16[32,2048]{1,0:T(8,128)(2,1)S(1)}, u32[]{:S(2)}, u32[]{:S(2)}) %collective-permute-start) | collective-permute-done | bytes 131104 | tf_op jit(solution)/shard_map/while/body/eval_jaxpr/ppermute | solution.py:17
  303.7 1.5 fusion.35
  309.9 4.6 %collective-permute-done = bf16[32,2048]{1,0:T(8,128)(2,1)S(1)} collective-permute-done((bf16[32,2048]{1,0:T(8,128)(2,1)S(1)}, bf16[32,2048]{1,0:T(8,128)(2,1)S(1)}, u32[]{:S(2)}, u32[]{:S(2)}) %collective-permute-start) | collective-permute-done | bytes 131104 | tf_op jit(solution)/shard_map/while/body/eval_jaxpr/ppermute | solution.py:17
  315.1 1.5 fusion.35
  321.3 4.6 %collective-permute-done = bf16[32,2048]{1,0:T(8,128)(2,1)S(1)} collective-permute-done((bf16[32,2048]{1,0:T(8,128)(2,1)S(1)}, bf16[32,2048]{1,0:T(8,128)(2,1)S(1)}, u32[]{:S(2)}, u32[]{:S(2)}) %collective-permute-start) | collective-permute-done | bytes 131104 | tf_op jit(solution)/shard_map/while/body/eval_jaxpr/ppermute | solution.py:17
  326.5 1.5 fusion.35
  332.7 4.6 %collective-permute-done = bf16[32,2048]{1,0:T(8,128)(2,1)S(1)} collective-permute-done((bf16[32,2048]{1,0:T(8,128)(2,1)S(1)}, bf16[32,2048]{1,0:T(8,128)(2,1)S(1)}, u32[]{:S(2)}, u32[]{:S(2)}) %collective-permute-start) | collective-permute-done | bytes 131104 | tf_op jit(solution)/shard_map/while/body/eval_jaxpr/ppermute | solution.py:17
  337.9 1.5 fusion.35
  344.1 4.6 %collective-permute-done = bf16[32,2048]{1,0:T(8,128)(2,1)S(1)} collective-permute-done((bf16[32,2048]{1,0:T(8,128)(2,1)S(1)}, bf16[32,2048]{1,0:T(8,128)(2,1)S(1)}, u32[]{:S(2)}, u32[]{:S(2)}) %collective-permute-start) | collective-permute-done | bytes 131104 | tf_op jit(solution)/shard_map/while/body/eval_jaxpr/ppermute | solution.py:17
  349.3 1.5 fusion.35
  355.5 4.7 %collective-permute-done = bf16[32,2048]{1,0:T(8,128)(2,1)S(1)} collective-permute-done((bf16[32,2048]{1,0:T(8,128)(2,1)S(1)}, bf16[32,2048]{1,0:T(8,128)(2,1)S(1)}, u32[]{:S(2)}, u32[]{:S(2)}) %collective-permute-start) | collective-permute-done | bytes 131104 | tf_op jit(solution)/shard_map/while/body/eval_jaxpr/ppermute | solution.py:17
  364.7 5.9 %all-to-all-start = ((bf16[8,32,2048]{2,1,0:T(8,128)(2,1)}), bf16[8,32,2048]{2,1,0:T(8,128)(2,1)S(1)}, u32[]{:S(2)}, u32[]{:S(2)}) async-start(bf16[8,32,2048]{2,1,0:T(8,128)(2,1)} %stack.2), calls=%async_computation | async-start | bytes 2097152 | tf_op jit(solution)/shard_map/all_to_all | solution.py:11
  370.6 10.0 %all-to-all-done = bf16[8,32,2048]{2,1,0:T(8,128)(2,1)S(1)} async-done(((bf16[8,32,2048]{2,1,0:T(8,128)(2,1)}), bf16[8,32,2048]{2,1,0:T(8,128)(2,1)S(1)}, u32[]{:S(2)}, u32[]{:S(2)}) %all-to-all-start) | async-done | bytes 1048608 | tf_op jit(solution)/shard_map/all_to_all | solution.py:11
  (359 shorter events, 157.7 us)
Async XLA Ops:
  0.0 380.6 %copy-start = (bf16[256,256]{1,0:T(8,128)(2,1)S(1)}, bf16[256,256]{1,0:T(8,128)(2,1)}, u32[]{:S(2)}) copy-start(bf16[256,256]{1,0:T(8,128)(2,1)} %param.15) | copy-start | bytes 393220
  8.5 9.6 %collective-permute-start = (bf16[32,2048]{1,0:T(8,128)(2,1)S(1)}, bf16[32,2048]{1,0:T(8,128)(2,1)S(1)}, u32[]{:S(2)}, u32[]{:S(2)}) collective-permute-start(bf16[32,2048]{1,0:T(8,128)(2,1)S(1)} %get-tuple-element.350), channel_id=1, source_target_pairs={{248,0},{0,8},{8,16},{16,24},{24,32},{32,40},{40,48},{48,56},{56,6... | collective-permute-start | bytes 393224 | tf_op jit(solution)/shard_map/while/body/eval_jaxpr/ppermute | solution.py:17
  21.4 8.1 %collective-permute-start = (bf16[32,2048]{1,0:T(8,128)(2,1)S(1)}, bf16[32,2048]{1,0:T(8,128)(2,1)S(1)}, u32[]{:S(2)}, u32[]{:S(2)}) collective-permute-start(bf16[32,2048]{1,0:T(8,128)(2,1)S(1)} %get-tuple-element.350), channel_id=1, source_target_pairs={{248,0},{0,8},{8,16},{16,24},{24,32},{32,40},{40,48},{48,56},{56,6... | collective-permute-start | bytes 393224 | tf_op jit(solution)/shard_map/while/body/eval_jaxpr/ppermute | solution.py:17
  32.8 8.1 %collective-permute-start = (bf16[32,2048]{1,0:T(8,128)(2,1)S(1)}, bf16[32,2048]{1,0:T(8,128)(2,1)S(1)}, u32[]{:S(2)}, u32[]{:S(2)}) collective-permute-start(bf16[32,2048]{1,0:T(8,128)(2,1)S(1)} %get-tuple-element.350), channel_id=1, source_target_pairs={{248,0},{0,8},{8,16},{16,24},{24,32},{32,40},{40,48},{48,56},{56,6... | collective-permute-start | bytes 393224 | tf_op jit(solution)/shard_map/while/body/eval_jaxpr/ppermute | solution.py:17
  44.2 8.1 %collective-permute-start = (bf16[32,2048]{1,0:T(8,128)(2,1)S(1)}, bf16[32,2048]{1,0:T(8,128)(2,1)S(1)}, u32[]{:S(2)}, u32[]{:S(2)}) collective-permute-start(bf16[32,2048]{1,0:T(8,128)(2,1)S(1)} %get-tuple-element.350), channel_id=1, source_target_pairs={{248,0},{0,8},{8,16},{16,24},{24,32},{32,40},{40,48},{48,56},{56,6... | collective-permute-start | bytes 393224 | tf_op jit(solution)/shard_map/while/body/eval_jaxpr/ppermute | solution.py:17
  55.6 8.1 %collective-permute-start = (bf16[32,2048]{1,0:T(8,128)(2,1)S(1)}, bf16[32,2048]{1,0:T(8,128)(2,1)S(1)}, u32[]{:S(2)}, u32[]{:S(2)}) collective-permute-start(bf16[32,2048]{1,0:T(8,128)(2,1)S(1)} %get-tuple-element.350), channel_id=1, source_target_pairs={{248,0},{0,8},{8,16},{16,24},{24,32},{32,40},{40,48},{48,56},{56,6... | collective-permute-start | bytes 393224 | tf_op jit(solution)/shard_map/while/body/eval_jaxpr/ppermute | solution.py:17
  67.0 8.1 %collective-permute-start = (bf16[32,2048]{1,0:T(8,128)(2,1)S(1)}, bf16[32,2048]{1,0:T(8,128)(2,1)S(1)}, u32[]{:S(2)}, u32[]{:S(2)}) collective-permute-start(bf16[32,2048]{1,0:T(8,128)(2,1)S(1)} %get-tuple-element.350), channel_id=1, source_target_pairs={{248,0},{0,8},{8,16},{16,24},{24,32},{32,40},{40,48},{48,56},{56,6... | collective-permute-start | bytes 393224 | tf_op jit(solution)/shard_map/while/body/eval_jaxpr/ppermute | solution.py:17
  78.4 8.1 %collective-permute-start = (bf16[32,2048]{1,0:T(8,128)(2,1)S(1)}, bf16[32,2048]{1,0:T(8,128)(2,1)S(1)}, u32[]{:S(2)}, u32[]{:S(2)}) collective-permute-start(bf16[32,2048]{1,0:T(8,128)(2,1)S(1)} %get-tuple-element.350), channel_id=1, source_target_pairs={{248,0},{0,8},{8,16},{16,24},{24,32},{32,40},{40,48},{48,56},{56,6... | collective-permute-start | bytes 393224 | tf_op jit(solution)/shard_map/while/body/eval_jaxpr/ppermute | solution.py:17
  89.8 8.1 %collective-permute-start = (bf16[32,2048]{1,0:T(8,128)(2,1)S(1)}, bf16[32,2048]{1,0:T(8,128)(2,1)S(1)}, u32[]{:S(2)}, u32[]{:S(2)}) collective-permute-start(bf16[32,2048]{1,0:T(8,128)(2,1)S(1)} %get-tuple-element.350), channel_id=1, source_target_pairs={{248,0},{0,8},{8,16},{16,24},{24,32},{32,40},{40,48},{48,56},{56,6... | collective-permute-start | bytes 393224 | tf_op jit(solution)/shard_map/while/body/eval_jaxpr/ppermute | solution.py:17
  101.2 8.1 %collective-permute-start = (bf16[32,2048]{1,0:T(8,128)(2,1)S(1)}, bf16[32,2048]{1,0:T(8,128)(2,1)S(1)}, u32[]{:S(2)}, u32[]{:S(2)}) collective-permute-start(bf16[32,2048]{1,0:T(8,128)(2,1)S(1)} %get-tuple-element.350), channel_id=1, source_target_pairs={{248,0},{0,8},{8,16},{16,24},{24,32},{32,40},{40,48},{48,56},{56,6... | collective-permute-start | bytes 393224 | tf_op jit(solution)/shard_map/while/body/eval_jaxpr/ppermute | solution.py:17
  112.6 8.1 %collective-permute-start = (bf16[32,2048]{1,0:T(8,128)(2,1)S(1)}, bf16[32,2048]{1,0:T(8,128)(2,1)S(1)}, u32[]{:S(2)}, u32[]{:S(2)}) collective-permute-start(bf16[32,2048]{1,0:T(8,128)(2,1)S(1)} %get-tuple-element.350), channel_id=1, source_target_pairs={{248,0},{0,8},{8,16},{16,24},{24,32},{32,40},{40,48},{48,56},{56,6... | collective-permute-start | bytes 393224 | tf_op jit(solution)/shard_map/while/body/eval_jaxpr/ppermute | solution.py:17
  124.0 8.1 %collective-permute-start = (bf16[32,2048]{1,0:T(8,128)(2,1)S(1)}, bf16[32,2048]{1,0:T(8,128)(2,1)S(1)}, u32[]{:S(2)}, u32[]{:S(2)}) collective-permute-start(bf16[32,2048]{1,0:T(8,128)(2,1)S(1)} %get-tuple-element.350), channel_id=1, source_target_pairs={{248,0},{0,8},{8,16},{16,24},{24,32},{32,40},{40,48},{48,56},{56,6... | collective-permute-start | bytes 393224 | tf_op jit(solution)/shard_map/while/body/eval_jaxpr/ppermute | solution.py:17
  135.4 8.1 %collective-permute-start = (bf16[32,2048]{1,0:T(8,128)(2,1)S(1)}, bf16[32,2048]{1,0:T(8,128)(2,1)S(1)}, u32[]{:S(2)}, u32[]{:S(2)}) collective-permute-start(bf16[32,2048]{1,0:T(8,128)(2,1)S(1)} %get-tuple-element.350), channel_id=1, source_target_pairs={{248,0},{0,8},{8,16},{16,24},{24,32},{32,40},{40,48},{48,56},{56,6... | collective-permute-start | bytes 393224 | tf_op jit(solution)/shard_map/while/body/eval_jaxpr/ppermute | solution.py:17
  146.8 8.1 %collective-permute-start = (bf16[32,2048]{1,0:T(8,128)(2,1)S(1)}, bf16[32,2048]{1,0:T(8,128)(2,1)S(1)}, u32[]{:S(2)}, u32[]{:S(2)}) collective-permute-start(bf16[32,2048]{1,0:T(8,128)(2,1)S(1)} %get-tuple-element.350), channel_id=1, source_target_pairs={{248,0},{0,8},{8,16},{16,24},{24,32},{32,40},{40,48},{48,56},{56,6... | collective-permute-start | bytes 393224 | tf_op jit(solution)/shard_map/while/body/eval_jaxpr/ppermute | solution.py:17
  158.2 8.1 %collective-permute-start = (bf16[32,2048]{1,0:T(8,128)(2,1)S(1)}, bf16[32,2048]{1,0:T(8,128)(2,1)S(1)}, u32[]{:S(2)}, u32[]{:S(2)}) collective-permute-start(bf16[32,2048]{1,0:T(8,128)(2,1)S(1)} %get-tuple-element.350), channel_id=1, source_target_pairs={{248,0},{0,8},{8,16},{16,24},{24,32},{32,40},{40,48},{48,56},{56,6... | collective-permute-start | bytes 393224 | tf_op jit(solution)/shard_map/while/body/eval_jaxpr/ppermute | solution.py:17
  169.6 8.1 %collective-permute-start = (bf16[32,2048]{1,0:T(8,128)(2,1)S(1)}, bf16[32,2048]{1,0:T(8,128)(2,1)S(1)}, u32[]{:S(2)}, u32[]{:S(2)}) collective-permute-start(bf16[32,2048]{1,0:T(8,128)(2,1)S(1)} %get-tuple-element.350), channel_id=1, source_target_pairs={{248,0},{0,8},{8,16},{16,24},{24,32},{32,40},{40,48},{48,56},{56,6... | collective-permute-start | bytes 393224 | tf_op jit(solution)/shard_map/while/body/eval_jaxpr/ppermute | solution.py:17
  180.9 8.1 %collective-permute-start = (bf16[32,2048]{1,0:T(8,128)(2,1)S(1)}, bf16[32,2048]{1,0:T(8,128)(2,1)S(1)}, u32[]{:S(2)}, u32[]{:S(2)}) collective-permute-start(bf16[32,2048]{1,0:T(8,128)(2,1)S(1)} %get-tuple-element.350), channel_id=1, source_target_pairs={{248,0},{0,8},{8,16},{16,24},{24,32},{32,40},{40,48},{48,56},{56,6... | collective-permute-start | bytes 393224 | tf_op jit(solution)/shard_map/while/body/eval_jaxpr/ppermute | solution.py:17
  192.3 8.1 %collective-permute-start = (bf16[32,2048]{1,0:T(8,128)(2,1)S(1)}, bf16[32,2048]{1,0:T(8,128)(2,1)S(1)}, u32[]{:S(2)}, u32[]{:S(2)}) collective-permute-start(bf16[32,2048]{1,0:T(8,128)(2,1)S(1)} %get-tuple-element.350), channel_id=1, source_target_pairs={{248,0},{0,8},{8,16},{16,24},{24,32},{32,40},{40,48},{48,56},{56,6... | collective-permute-start | bytes 393224 | tf_op jit(solution)/shard_map/while/body/eval_jaxpr/ppermute | solution.py:17
  203.7 8.1 %collective-permute-start = (bf16[32,2048]{1,0:T(8,128)(2,1)S(1)}, bf16[32,2048]{1,0:T(8,128)(2,1)S(1)}, u32[]{:S(2)}, u32[]{:S(2)}) collective-permute-start(bf16[32,2048]{1,0:T(8,128)(2,1)S(1)} %get-tuple-element.350), channel_id=1, source_target_pairs={{248,0},{0,8},{8,16},{16,24},{24,32},{32,40},{40,48},{48,56},{56,6... | collective-permute-start | bytes 393224 | tf_op jit(solution)/shard_map/while/body/eval_jaxpr/ppermute | solution.py:17
  215.2 8.1 %collective-permute-start = (bf16[32,2048]{1,0:T(8,128)(2,1)S(1)}, bf16[32,2048]{1,0:T(8,128)(2,1)S(1)}, u32[]{:S(2)}, u32[]{:S(2)}) collective-permute-start(bf16[32,2048]{1,0:T(8,128)(2,1)S(1)} %get-tuple-element.350), channel_id=1, source_target_pairs={{248,0},{0,8},{8,16},{16,24},{24,32},{32,40},{40,48},{48,56},{56,6... | collective-permute-start | bytes 393224 | tf_op jit(solution)/shard_map/while/body/eval_jaxpr/ppermute | solution.py:17
  226.6 8.1 %collective-permute-start = (bf16[32,2048]{1,0:T(8,128)(2,1)S(1)}, bf16[32,2048]{1,0:T(8,128)(2,1)S(1)}, u32[]{:S(2)}, u32[]{:S(2)}) collective-permute-start(bf16[32,2048]{1,0:T(8,128)(2,1)S(1)} %get-tuple-element.350), channel_id=1, source_target_pairs={{248,0},{0,8},{8,16},{16,24},{24,32},{32,40},{40,48},{48,56},{56,6... | collective-permute-start | bytes 393224 | tf_op jit(solution)/shard_map/while/body/eval_jaxpr/ppermute | solution.py:17
  238.0 8.1 %collective-permute-start = (bf16[32,2048]{1,0:T(8,128)(2,1)S(1)}, bf16[32,2048]{1,0:T(8,128)(2,1)S(1)}, u32[]{:S(2)}, u32[]{:S(2)}) collective-permute-start(bf16[32,2048]{1,0:T(8,128)(2,1)S(1)} %get-tuple-element.350), channel_id=1, source_target_pairs={{248,0},{0,8},{8,16},{16,24},{24,32},{32,40},{40,48},{48,56},{56,6... | collective-permute-start | bytes 393224 | tf_op jit(solution)/shard_map/while/body/eval_jaxpr/ppermute | solution.py:17
  249.4 8.1 %collective-permute-start = (bf16[32,2048]{1,0:T(8,128)(2,1)S(1)}, bf16[32,2048]{1,0:T(8,128)(2,1)S(1)}, u32[]{:S(2)}, u32[]{:S(2)}) collective-permute-start(bf16[32,2048]{1,0:T(8,128)(2,1)S(1)} %get-tuple-element.350), channel_id=1, source_target_pairs={{248,0},{0,8},{8,16},{16,24},{24,32},{32,40},{40,48},{48,56},{56,6... | collective-permute-start | bytes 393224 | tf_op jit(solution)/shard_map/while/body/eval_jaxpr/ppermute | solution.py:17
  260.8 8.1 %collective-permute-start = (bf16[32,2048]{1,0:T(8,128)(2,1)S(1)}, bf16[32,2048]{1,0:T(8,128)(2,1)S(1)}, u32[]{:S(2)}, u32[]{:S(2)}) collective-permute-start(bf16[32,2048]{1,0:T(8,128)(2,1)S(1)} %get-tuple-element.350), channel_id=1, source_target_pairs={{248,0},{0,8},{8,16},{16,24},{24,32},{32,40},{40,48},{48,56},{56,6... | collective-permute-start | bytes 393224 | tf_op jit(solution)/shard_map/while/body/eval_jaxpr/ppermute | solution.py:17
  272.2 8.1 %collective-permute-start = (bf16[32,2048]{1,0:T(8,128)(2,1)S(1)}, bf16[32,2048]{1,0:T(8,128)(2,1)S(1)}, u32[]{:S(2)}, u32[]{:S(2)}) collective-permute-start(bf16[32,2048]{1,0:T(8,128)(2,1)S(1)} %get-tuple-element.350), channel_id=1, source_target_pairs={{248,0},{0,8},{8,16},{16,24},{24,32},{32,40},{40,48},{48,56},{56,6... | collective-permute-start | bytes 393224 | tf_op jit(solution)/shard_map/while/body/eval_jaxpr/ppermute | solution.py:17
  283.6 8.1 %collective-permute-start = (bf16[32,2048]{1,0:T(8,128)(2,1)S(1)}, bf16[32,2048]{1,0:T(8,128)(2,1)S(1)}, u32[]{:S(2)}, u32[]{:S(2)}) collective-permute-start(bf16[32,2048]{1,0:T(8,128)(2,1)S(1)} %get-tuple-element.350), channel_id=1, source_target_pairs={{248,0},{0,8},{8,16},{16,24},{24,32},{32,40},{40,48},{48,56},{56,6... | collective-permute-start | bytes 393224 | tf_op jit(solution)/shard_map/while/body/eval_jaxpr/ppermute | solution.py:17
  295.0 8.1 %collective-permute-start = (bf16[32,2048]{1,0:T(8,128)(2,1)S(1)}, bf16[32,2048]{1,0:T(8,128)(2,1)S(1)}, u32[]{:S(2)}, u32[]{:S(2)}) collective-permute-start(bf16[32,2048]{1,0:T(8,128)(2,1)S(1)} %get-tuple-element.350), channel_id=1, source_target_pairs={{248,0},{0,8},{8,16},{16,24},{24,32},{32,40},{40,48},{48,56},{56,6... | collective-permute-start | bytes 393224 | tf_op jit(solution)/shard_map/while/body/eval_jaxpr/ppermute | solution.py:17
  306.4 8.1 %collective-permute-start = (bf16[32,2048]{1,0:T(8,128)(2,1)S(1)}, bf16[32,2048]{1,0:T(8,128)(2,1)S(1)}, u32[]{:S(2)}, u32[]{:S(2)}) collective-permute-start(bf16[32,2048]{1,0:T(8,128)(2,1)S(1)} %get-tuple-element.350), channel_id=1, source_target_pairs={{248,0},{0,8},{8,16},{16,24},{24,32},{32,40},{40,48},{48,56},{56,6... | collective-permute-start | bytes 393224 | tf_op jit(solution)/shard_map/while/body/eval_jaxpr/ppermute | solution.py:17
  317.8 8.1 %collective-permute-start = (bf16[32,2048]{1,0:T(8,128)(2,1)S(1)}, bf16[32,2048]{1,0:T(8,128)(2,1)S(1)}, u32[]{:S(2)}, u32[]{:S(2)}) collective-permute-start(bf16[32,2048]{1,0:T(8,128)(2,1)S(1)} %get-tuple-element.350), channel_id=1, source_target_pairs={{248,0},{0,8},{8,16},{16,24},{24,32},{32,40},{40,48},{48,56},{56,6... | collective-permute-start | bytes 393224 | tf_op jit(solution)/shard_map/while/body/eval_jaxpr/ppermute | solution.py:17
  329.2 8.1 %collective-permute-start = (bf16[32,2048]{1,0:T(8,128)(2,1)S(1)}, bf16[32,2048]{1,0:T(8,128)(2,1)S(1)}, u32[]{:S(2)}, u32[]{:S(2)}) collective-permute-start(bf16[32,2048]{1,0:T(8,128)(2,1)S(1)} %get-tuple-element.350), channel_id=1, source_target_pairs={{248,0},{0,8},{8,16},{16,24},{24,32},{32,40},{40,48},{48,56},{56,6... | collective-permute-start | bytes 393224 | tf_op jit(solution)/shard_map/while/body/eval_jaxpr/ppermute | solution.py:17
  340.6 8.1 %collective-permute-start = (bf16[32,2048]{1,0:T(8,128)(2,1)S(1)}, bf16[32,2048]{1,0:T(8,128)(2,1)S(1)}, u32[]{:S(2)}, u32[]{:S(2)}) collective-permute-start(bf16[32,2048]{1,0:T(8,128)(2,1)S(1)} %get-tuple-element.350), channel_id=1, source_target_pairs={{248,0},{0,8},{8,16},{16,24},{24,32},{32,40},{40,48},{48,56},{56,6... | collective-permute-start | bytes 393224 | tf_op jit(solution)/shard_map/while/body/eval_jaxpr/ppermute | solution.py:17
  352.0 8.2 %collective-permute-start = (bf16[32,2048]{1,0:T(8,128)(2,1)S(1)}, bf16[32,2048]{1,0:T(8,128)(2,1)S(1)}, u32[]{:S(2)}, u32[]{:S(2)}) collective-permute-start(bf16[32,2048]{1,0:T(8,128)(2,1)S(1)} %get-tuple-element.350), channel_id=1, source_target_pairs={{248,0},{0,8},{8,16},{16,24},{24,32},{32,40},{40,48},{48,56},{56,6... | collective-permute-start | bytes 393224 | tf_op jit(solution)/shard_map/while/body/eval_jaxpr/ppermute | solution.py:17
  364.7 16.0 %all-to-all-start = ((bf16[8,32,2048]{2,1,0:T(8,128)(2,1)}), bf16[8,32,2048]{2,1,0:T(8,128)(2,1)S(1)}, u32[]{:S(2)}, u32[]{:S(2)}) async-start(bf16[8,32,2048]{2,1,0:T(8,128)(2,1)} %stack.2), calls=%async_computation | async-start | bytes 2097152 | tf_op jit(solution)/shard_map/all_to_all | solution.py:11
